TPU v7x, 32 devices: a whole 2x2x4 slice. The times are simulated.
32 devices in a mesh: ctx: 16 (over z, y, core), grp: 2 (over x).
Axes of the slice: x: 2, y: 2, z: 4, core: 2. Of those that a mesh axis runs over, the one named last changes fastest.
Arguments:
- query_in: bfloat16 [2560, 768], P(('grp', 'ctx')), parts along dimension 0, may hold values from -30 to 30
- key_in: bfloat16 [2560, 768], P(('grp', 'ctx')), parts along dimension 0, may hold values from -6 to 6
- value_in: bfloat16 [2560, 768], P(('grp', 'ctx')), parts along dimension 0, may hold values from -6 to 6
- length: int32 [2], P('grp'), parts along dimension 0, may hold values from 320 to 1280
- out_weight: bfloat16 [768, 1536], replicated, may hold values from -0.21875 to 0.21875
Outputs:
- projected: bfloat16 [2560, 1536], P(('grp', 'ctx')), parts along dimension 0
There are 2 independent parts, one for each index of `grp`. A program takes and returns all parts, laid end to end along the dimension named above; an argument that names none is the same for every part. Nothing has to cross between parts.
All inputs are finite; a program needn't handle non-finite values.
Results may differ from a plain program's by a relative error of at most 0.007.
Values may be sent and summed in bfloat16 or wider, within the bound.
A program may use at most 64 MiB of HBM per device.

v0:
```python
import jax
import jax.numpy as jnp
from jax import lax
from jax.sharding import PartitionSpec as P

HEADS = 12
HDIM = 64


def body(query_in, key_in, value_in, length, out_weight):
    local_rows = query_in.shape[0]
    offset = lax.axis_index("ctx") * local_rows
    valid_len = length[0]
    score_scale = 1.0 / jnp.sqrt(jnp.float32(HDIM))
    query_heads = query_in.reshape(local_rows, HEADS, HDIM).transpose(1, 0, 2)
    start_state = (
        jnp.full((HEADS, local_rows), -1e30, jnp.float32),
        jnp.zeros((HEADS, local_rows), jnp.float32),
        jnp.zeros((HEADS, local_rows, HDIM), jnp.float32),
    )
    key_part = lax.all_gather(key_in, "ctx", axis=0, tiled=True)
    value_part = lax.all_gather(value_in, "ctx", axis=0, tiled=True)
    part_rows = key_part.shape[0]
    key_live = (jnp.arange(part_rows, dtype=jnp.int32) < valid_len)[None, :]
    key_heads = key_part.reshape(part_rows, HEADS, HDIM).transpose(1, 0, 2)
    value_heads = value_part.reshape(part_rows, HEADS, HDIM).transpose(1, 0, 2)

    def fold_head(operands):
        query_h, key_h, value_h, run_max, run_sum, run_acc = operands
        scores = jnp.dot(query_h, key_h.T, preferred_element_type=jnp.float32) * score_scale
        new_max = jnp.maximum(
            run_max, jnp.max(jnp.where(key_live, scores, jnp.float32(-1e30)), axis=1)
        )
        expons = jnp.where(key_live, jnp.exp(scores - new_max[:, None]), jnp.float32(0.0))
        factor = jnp.exp(run_max - new_max)
        added = jnp.dot(expons.astype(jnp.bfloat16), value_h, preferred_element_type=jnp.float32)
        return (
            new_max,
            run_sum * factor + jnp.sum(expons, axis=1),
            run_acc * factor[:, None] + added,
        )

    running, denominator, weighted = lax.map(
        fold_head, (query_heads, key_heads, value_heads) + tuple(start_state)
    )
    heads_out = (
        (weighted / denominator[:, :, None]).transpose(1, 0, 2).reshape(local_rows, HEADS * HDIM)
    )
    query_live = offset + jnp.arange(local_rows, dtype=jnp.int32) < valid_len
    attended = jnp.where(query_live[:, None], heads_out, jnp.float32(0.0)).astype(jnp.bfloat16)
    return jnp.dot(attended, out_weight, preferred_element_type=jnp.float32).astype(jnp.bfloat16)


def solution(mesh):
    in_specs = (
        P(("grp", "ctx"), None),
        P(("grp", "ctx"), None),
        P(("grp", "ctx"), None),
        P("grp"),
        P(),
    )
    out_specs = P(("grp", "ctx"), None)
    return jax.shard_map(body, mesh=mesh, in_specs=in_specs, out_specs=out_specs, check_vma=False)
```

profile of v0, /device:TPU:0, one launch (start us, length us, event | category | flops | bytes accessed | tf_op | source)
XLA Modules:
  0.0 149.1 jit_solution(4521468957374590369)
XLA Ops:
  6.5 0.0 copy-start
  6.5 0.0 all-gather.3.cloned.1.call-start
  6.5 0.7 all-gather.3.cloned.1.call-update
  7.3 0.0 all-gather.5.cloned.1.call-start
  7.3 0.7 all-gather.5.cloned.1.call-update
  8.0 1.1 copy.12
  9.8 43.4 %all-gather.3.cloned.1.call-done = bf16[1280,768]{1,0:T(8,128)(2,1)} async-done(((bf16[80,768]{1,0:T(8,128)(2,1)}), bf16[1280,768]{1,0:T(8,128)(2,1)}) %all-gather.3.cloned.1.call-update) | async-done | bytes 1966096 | tf_op jit(solution)/shard_map/all_gather | solution.py:21
  53.2 4.0 %copy.13 = bf16[1280,768]{0,1:T(8,128)(2,1)} copy(bf16[1280,768]{1,0:T(8,128)(2,1)} %all-gather.3.cloned.1.call-done) | data formatting | bytes 3932160 | tf_op jit(solution)/shard_map/all_gather | solution.py:21
  57.2 38.1 %all-gather.5.cloned.1.call-done = bf16[1280,768]{1,0:T(8,128)(2,1)} async-done(((bf16[80,768]{1,0:T(8,128)(2,1)}), bf16[1280,768]{1,0:T(8,128)(2,1)}) %all-gather.5.cloned.1.call-update) | async-done | bytes 1966096 | tf_op jit(solution)/shard_map/all_gather | solution.py:22
  95.3 4.0 %copy.14 = bf16[1280,768]{0,1:T(8,128)(2,1)} copy(bf16[1280,768]{1,0:T(8,128)(2,1)} %all-gather.5.cloned.1.call-done) | data formatting | bytes 3932160 | tf_op jit(solution)/shard_map/all_gather | solution.py:22
  99.3 41.6 %while.13 = (s32[]{:T(128)}, f32[12,80]{1,0:T(8,128)S(1)}, f32[12,80,64]{1,2,0:T(8,128)S(1)}, bf16[12,80,64]{1,2,0:T(8,128)(2,1)S(1)}, bf16[12,1280,64]{1,2,0:T(...) while((s32[]{:T(128)}, f32[12,80]{1,0:T(8,128)S(1)}, ...), condition=%wide.region_3.4_spmd.clone, body=%wide.region_0.3_spmd.clone.sunk | while | flops 27142640 | bytes 1618981 | solution.py:43
  99.3 0.7 compare_reduce_fusion.2
  100.0 1.3 select_reduce_fusion.2
  101.2 0.2 fusion.28
  101.5 1.2 fusion.29
  102.7 0.7 compare_reduce_fusion.2
  103.4 1.3 select_reduce_fusion.2
  104.7 0.2 fusion.28
  105.0 1.2 fusion.29
  106.2 0.7 compare_reduce_fusion.2
  106.9 1.3 select_reduce_fusion.2
  108.2 0.2 fusion.28
  108.4 1.2 fusion.29
  109.7 0.7 compare_reduce_fusion.2
  110.4 1.3 select_reduce_fusion.2
  111.6 0.2 fusion.28
  111.9 1.2 fusion.29
  113.2 0.7 compare_reduce_fusion.2
  113.8 1.3 select_reduce_fusion.2
  115.1 0.2 fusion.28
  115.4 1.2 fusion.29
  116.6 0.7 compare_reduce_fusion.2
  117.3 1.3 select_reduce_fusion.2
  118.6 0.2 fusion.28
  118.8 1.2 fusion.29
  120.1 0.7 compare_reduce_fusion.2
  120.8 1.3 select_reduce_fusion.2
  122.1 0.2 fusion.28
  122.3 1.2 fusion.29
  123.6 0.7 compare_reduce_fusion.2
  124.2 1.3 select_reduce_fusion.2
  125.5 0.2 fusion.28
  125.8 1.2 fusion.29
  127.0 0.7 compare_reduce_fusion.2
  127.7 1.3 select_reduce_fusion.2
  129.0 0.2 fusion.28
  129.2 1.2 fusion.29
  130.5 0.7 compare_reduce_fusion.2
  131.2 1.3 select_reduce_fusion.2
  132.5 0.2 fusion.28
  132.7 1.2 fusion.29
  134.0 0.7 compare_reduce_fusion.2
  134.7 1.3 select_reduce_fusion.2
  135.9 0.2 fusion.28
  136.2 1.2 fusion.29
  137.4 0.7 compare_reduce_fusion.2
  138.1 1.3 select_reduce_fusion.2
  139.4 0.2 fusion.28
  139.7 1.2 fusion.29
  141.0 0.1 fusion.19
  141.0 0.0 copy-done
  141.0 1.3 convolution_convert_fusion
  (40 shorter events, 0.7 us)
Async XLA Ops:
  6.5 134.5 %copy-start = (bf16[768,1536]{1,0:T(8,128)(2,1)S(1)}, bf16[768,1536]{1,0:T(8,128)(2,1)}, u32[]{:S(2)}) copy-start(bf16[768,1536]{1,0:T(8,128)(2,1)} %param.11) | copy-start | bytes 7077892
  6.5 46.7 %all-gather.3.cloned.1.call-start = ((), (), s32[]{:S(2)}) async-start(), calls=%async_computation | async-start | bytes 2088960 | tf_op jit(solution)/shard_map/all_gather | solution.py:21
  7.3 88.0 %all-gather.5.cloned.1.call-start = ((), (), s32[]{:S(2)}) async-start(), calls=%async_computation.1 | async-start | bytes 2088960 | tf_op jit(solution)/shard_map/all_gather | solution.py:22
Sparse Core Ops, SparseCore 0:
  9.6 43.5 all-gather.2
  55.5 39.7 all-gather.4
where the time goes:
time: 150 us; the launch traced here: 149 us
  waiting for transfers between devices  82.9 us (55%)
  matrix products  30.9 us (21%)
  between operations  14.1 us (9%)
  other arithmetic  11.3 us (8%)
  local copies, waits for them, and re-layouts  9.49 us (6%)
    all_gather x1, waiting for transfers between devices, body(): key_part = lax.all_gather(key_in, 'ctx', axis=0, tiled=True)  43.4 us
    all_gather x1, waiting for transfers between devices, body(): value_part = lax.all_gather(value_in, 'ctx', axis=0, tiled=True)  38.1 us
    dot_general x12, matrix products, fold_head(): jnp.dot(query_h, key_h.T, preferred_element_type=jnp.float32) * score_scale  15.2 us
    dot_general x12, matrix products, fold_head(): jnp.dot(expons.astype(jnp.bfloat16), value_h, preferred_element_type=jnp....  14.4 us
    lt x12, other arithmetic, body(): key_live = (jnp.arange(part_rows, dtype=jnp.int32) < valid_len)[None, :]  8.16 us
    all_gather x1, local copies, waits for them, and re-layouts, body(): value_part = lax.all_gather(value_in, 'ctx', axis=0, tiled=True)  4 us
    all_gather x1, local copies, waits for them, and re-layouts, body(): key_part = lax.all_gather(key_in, 'ctx', axis=0, tiled=True)  3.97 us
  transfers between devices with their start and end apart: 2, of which 2 were waited for; matrix products, arithmetic and copies ran while one was open for 3% of the time, Pallas kernels for 0%

commit v1 on v0

--- a/solution.py
+++ b/solution.py
@@ -18,8 +18,11 @@
         jnp.zeros((HEADS, local_rows), jnp.float32),
         jnp.zeros((HEADS, local_rows, HDIM), jnp.float32),
     )
-    key_part = lax.all_gather(key_in, "ctx", axis=0, tiled=True)
-    value_part = lax.all_gather(value_in, "ctx", axis=0, tiled=True)
+    key_part, value_part = jnp.split(
+        lax.all_gather(jnp.concatenate([key_in, value_in], axis=1), "ctx", axis=0, tiled=True),
+        [key_in.shape[1]],
+        axis=1,
+    )
     part_rows = key_part.shape[0]
     key_live = (jnp.arange(part_rows, dtype=jnp.int32) < valid_len)[None, :]
     key_heads = key_part.reshape(part_rows, HEADS, HDIM).transpose(1, 0, 2)

time: 150 us -> 124 us (0.83)
  waiting for transfers between devices: 82.9 us -> 51 us
  local copies, waits for them, and re-layouts: 9.49 us -> 13.8 us
  other arithmetic: 11.3 us -> 13.1 us
    all_gather x2 -> x1, waiting for transfers between devices: 81.5 us -> 51 us  [body(): lax.all_gather(jnp.concatenate([key_in, value_in], axis=1), 'ctx', axis=0...]
    unnamed x3 -> x5, local copies, waits for them, and re-layouts: 1.07 us -> 9.04 us
    all_gather x2 -> x0, local copies, waits for them, and re-layouts: 7.96 us -> none  [the longest x1 4 us: body(): value_part = lax.all_gather(value_in, 'ctx', axis=0, tiled=True)]
    split x0 -> x1, local copies, waits for them, and re-layouts: none -> 4.29 us  [body(): jnp.split(lax.all_gather(jnp.concatenate([key_in, value_in], axis=1), 'ct...]
    concatenate x0 -> x1, other arithmetic: none -> 1.82 us  [body(): jnp.concatenate([key_in, value_in], axis=1)]
  transfers between devices with their start and end apart: 2 -> 1, of which waited for: 2 -> 1; matrix products, arithmetic and copies ran while one was open for 3% -> 1% of each run, Pallas kernels for 0% -> 0%
where the time goes in v1:
time: 124 us; the launch traced here: 123 us
  waiting for transfers between devices  51 us (41%)
  matrix products  30.9 us (25%)
  between operations  14.1 us (11%)
  local copies, waits for them, and re-layouts  13.8 us (11%)
  other arithmetic  13.1 us (11%)
    all_gather x1, waiting for transfers between devices, body(): lax.all_gather(jnp.concatenate([key_in, value_in], axis=1), 'ctx', axis=0...  51 us
    dot_general x12, matrix products, fold_head(): jnp.dot(query_h, key_h.T, preferred_element_type=jnp.float32) * score_scale  15.2 us
    dot_general x12, matrix products, fold_head(): jnp.dot(expons.astype(jnp.bfloat16), value_h, preferred_element_type=jnp....  14.4 us
    unnamed x5, local copies, waits for them, and re-layouts  9.04 us
    lt x12, other arithmetic, body(): key_live = (jnp.arange(part_rows, dtype=jnp.int32) < valid_len)[None, :]  8.16 us
    split x1, local copies, waits for them, and re-layouts, body(): jnp.split(lax.all_gather(jnp.concatenate([key_in, value_in], axis=1), 'ct...  4.29 us
    reduce_sum x12, other arithmetic, fold_head(): jnp.sum(expons, axis=1)  2.83 us
  transfers between devices with their start and end apart: 1, of which 1 were waited for; matrix products, arithmetic and copies ran while one was open for 1% of the time, Pallas kernels for 0%

profile of v1, /device:TPU:0, one launch (start us, length us, event | category | flops | bytes accessed | tf_op | source)
XLA Modules:
  0.0 123.3 jit_solution(4527870961797993651)
XLA Ops:
  6.5 0.0 copy-start
  6.5 0.0 all-gather.2.cloned.1.call-start
  6.5 1.8 %pad_maximum_fusion = bf16[80,1536]{1,0:T(8,128)(2,1)} fusion(bf16[80,768]{1,0:T(8,128)(2,1)} %param.9, bf16[80,768]{1,0:T(8,128)(2,1)} %param.8), kind=kLoop, calls=%fused_computation.28 | loop fusion | flops 491520 | bytes 491520 | tf_op jit(solution)/shard_map/concatenate | solution.py:22
  8.4 0.0 all-gather.2.cloned.1.call-update
  8.4 1.1 copy.12
  10.1 51.0 %all-gather.2.cloned.1.call-done = bf16[1280,1536]{1,0:T(8,128)(2,1)} async-done(((bf16[80,1536]{1,0:T(8,128)(2,1)}), bf16[1280,1536]{1,0:T(8,128)(2,1)}) %all-gather.2.cloned.1.call-update) | async-done | bytes 3932176 | tf_op jit(solution)/shard_map/all_gather | solution.py:22
  61.2 4.3 %fusion.20 = (bf16[1280,768]{1,0:T(8,128)(2,1)}, bf16[1280,768]{1,0:T(8,128)(2,1)}) fusion(bf16[1280,1536]{1,0:T(8,128)(2,1)} %all-gather.2.cloned.1.call-done), kind=kLoop, calls=%fused_computation.31 | loop fusion | bytes 7864320 | tf_op jit(solution)/shard_map/split | solution.py:21
  65.5 4.0 %copy.21 = bf16[1280,768]{0,1:T(8,128)(2,1)} copy(bf16[1280,768]{1,0:T(8,128)(2,1)} %get-tuple-element.95) | data formatting | bytes 3932160
  69.5 4.0 %copy.22 = bf16[1280,768]{0,1:T(8,128)(2,1)} copy(bf16[1280,768]{1,0:T(8,128)(2,1)} %get-tuple-element.94) | data formatting | bytes 3932160
  73.4 41.6 %while.13 = (s32[]{:T(128)}, f32[12,80]{1,0:T(8,128)S(1)}, f32[12,80,64]{1,2,0:T(8,128)S(1)}, bf16[12,80,64]{1,2,0:T(8,128)(2,1)S(1)}, bf16[12,1280,64]{1,2,0:T(...) while((s32[]{:T(128)}, f32[12,80]{1,0:T(8,128)S(1)}, ...), condition=%wide.region_3.4_spmd.clone, body=%wide.region_0.3_spmd.clone.sunk | while | flops 27142640 | bytes 1618981 | solution.py:46
  73.4 0.7 compare_reduce_fusion.2
  74.1 1.3 %select_reduce_fusion.2 = (f32[80]{0:T(128)S(1)}, f32[80,1280]{1,0:T(8,128)S(1)}) fusion(pred[1280]{0:T(1024)(128)(4,1)S(1)} %compare_reduce_fusion.2, bf16[12,1280,64]{1,2,0:T(8,128)(2,1)} %get-tuple-element.169, s32[]{:T(128)} %get-tuple-element.156, bf16[12,80,64]{1,2,0:T(8,128)(2,1)S(1)} %get-tuple-element.168), kind=kOutput, calls=%fused_computation.6.clone.1 | convolution fusion | flops 13414320 | bytes 593216 | tf_op jit(solution)/shard_map/while/body/eval_jaxpr/dot_general | solution.py:33
  75.4 0.2 fusion.29
  75.6 1.2 fusion.30
  76.9 0.7 compare_reduce_fusion.2
  77.6 1.3 %select_reduce_fusion.2 = (f32[80]{0:T(128)S(1)}, f32[80,1280]{1,0:T(8,128)S(1)}) fusion(pred[1280]{0:T(1024)(128)(4,1)S(1)} %compare_reduce_fusion.2, bf16[12,1280,64]{1,2,0:T(8,128)(2,1)} %get-tuple-element.169, s32[]{:T(128)} %get-tuple-element.156, bf16[12,80,64]{1,2,0:T(8,128)(2,1)S(1)} %get-tuple-element.168), kind=kOutput, calls=%fused_computation.6.clone.1 | convolution fusion | flops 13414320 | bytes 593216 | tf_op jit(solution)/shard_map/while/body/eval_jaxpr/dot_general | solution.py:33
  78.9 0.2 fusion.29
  79.1 1.2 fusion.30
  80.4 0.7 compare_reduce_fusion.2
  81.0 1.3 %select_reduce_fusion.2 = (f32[80]{0:T(128)S(1)}, f32[80,1280]{1,0:T(8,128)S(1)}) fusion(pred[1280]{0:T(1024)(128)(4,1)S(1)} %compare_reduce_fusion.2, bf16[12,1280,64]{1,2,0:T(8,128)(2,1)} %get-tuple-element.169, s32[]{:T(128)} %get-tuple-element.156, bf16[12,80,64]{1,2,0:T(8,128)(2,1)S(1)} %get-tuple-element.168), kind=kOutput, calls=%fused_computation.6.clone.1 | convolution fusion | flops 13414320 | bytes 593216 | tf_op jit(solution)/shard_map/while/body/eval_jaxpr/dot_general | solution.py:33
  82.3 0.2 fusion.29
  82.6 1.2 fusion.30
  83.8 0.7 compare_reduce_fusion.2
  84.5 1.3 %select_reduce_fusion.2 = (f32[80]{0:T(128)S(1)}, f32[80,1280]{1,0:T(8,128)S(1)}) fusion(pred[1280]{0:T(1024)(128)(4,1)S(1)} %compare_reduce_fusion.2, bf16[12,1280,64]{1,2,0:T(8,128)(2,1)} %get-tuple-element.169, s32[]{:T(128)} %get-tuple-element.156, bf16[12,80,64]{1,2,0:T(8,128)(2,1)S(1)} %get-tuple-element.168), kind=kOutput, calls=%fused_computation.6.clone.1 | convolution fusion | flops 13414320 | bytes 593216 | tf_op jit(solution)/shard_map/while/body/eval_jaxpr/dot_general | solution.py:33
  85.8 0.2 fusion.29
  86.0 1.2 fusion.30
  87.3 0.7 compare_reduce_fusion.2
  88.0 1.3 %select_reduce_fusion.2 = (f32[80]{0:T(128)S(1)}, f32[80,1280]{1,0:T(8,128)S(1)}) fusion(pred[1280]{0:T(1024)(128)(4,1)S(1)} %compare_reduce_fusion.2, bf16[12,1280,64]{1,2,0:T(8,128)(2,1)} %get-tuple-element.169, s32[]{:T(128)} %get-tuple-element.156, bf16[12,80,64]{1,2,0:T(8,128)(2,1)S(1)} %get-tuple-element.168), kind=kOutput, calls=%fused_computation.6.clone.1 | convolution fusion | flops 13414320 | bytes 593216 | tf_op jit(solution)/shard_map/while/body/eval_jaxpr/dot_general | solution.py:33
  89.3 0.2 fusion.29
  89.5 1.2 fusion.30
  90.8 0.7 compare_reduce_fusion.2
  91.5 1.3 %select_reduce_fusion.2 = (f32[80]{0:T(128)S(1)}, f32[80,1280]{1,0:T(8,128)S(1)}) fusion(pred[1280]{0:T(1024)(128)(4,1)S(1)} %compare_reduce_fusion.2, bf16[12,1280,64]{1,2,0:T(8,128)(2,1)} %get-tuple-element.169, s32[]{:T(128)} %get-tuple-element.156, bf16[12,80,64]{1,2,0:T(8,128)(2,1)S(1)} %get-tuple-element.168), kind=kOutput, calls=%fused_computation.6.clone.1 | convolution fusion | flops 13414320 | bytes 593216 | tf_op jit(solution)/shard_map/while/body/eval_jaxpr/dot_general | solution.py:33
  92.7 0.2 fusion.29
  93.0 1.2 fusion.30
  94.2 0.7 compare_reduce_fusion.2
  94.9 1.3 %select_reduce_fusion.2 = (f32[80]{0:T(128)S(1)}, f32[80,1280]{1,0:T(8,128)S(1)}) fusion(pred[1280]{0:T(1024)(128)(4,1)S(1)} %compare_reduce_fusion.2, bf16[12,1280,64]{1,2,0:T(8,128)(2,1)} %get-tuple-element.169, s32[]{:T(128)} %get-tuple-element.156, bf16[12,80,64]{1,2,0:T(8,128)(2,1)S(1)} %get-tuple-element.168), kind=kOutput, calls=%fused_computation.6.clone.1 | convolution fusion | flops 13414320 | bytes 593216 | tf_op jit(solution)/shard_map/while/body/eval_jaxpr/dot_general | solution.py:33
  96.2 0.2 fusion.29
  96.5 1.2 fusion.30
  97.7 0.7 compare_reduce_fusion.2
  98.4 1.3 %select_reduce_fusion.2 = (f32[80]{0:T(128)S(1)}, f32[80,1280]{1,0:T(8,128)S(1)}) fusion(pred[1280]{0:T(1024)(128)(4,1)S(1)} %compare_reduce_fusion.2, bf16[12,1280,64]{1,2,0:T(8,128)(2,1)} %get-tuple-element.169, s32[]{:T(128)} %get-tuple-element.156, bf16[12,80,64]{1,2,0:T(8,128)(2,1)S(1)} %get-tuple-element.168), kind=kOutput, calls=%fused_computation.6.clone.1 | convolution fusion | flops 13414320 | bytes 593216 | tf_op jit(solution)/shard_map/while/body/eval_jaxpr/dot_general | solution.py:33
  99.7 0.2 fusion.29
  99.9 1.2 fusion.30
  101.2 0.7 compare_reduce_fusion.2
  101.9 1.3 %select_reduce_fusion.2 = (f32[80]{0:T(128)S(1)}, f32[80,1280]{1,0:T(8,128)S(1)}) fusion(pred[1280]{0:T(1024)(128)(4,1)S(1)} %compare_reduce_fusion.2, bf16[12,1280,64]{1,2,0:T(8,128)(2,1)} %get-tuple-element.169, s32[]{:T(128)} %get-tuple-element.156, bf16[12,80,64]{1,2,0:T(8,128)(2,1)S(1)} %get-tuple-element.168), kind=kOutput, calls=%fused_computation.6.clone.1 | convolution fusion | flops 13414320 | bytes 593216 | tf_op jit(solution)/shard_map/while/body/eval_jaxpr/dot_general | solution.py:33
  103.1 0.2 fusion.29
  103.4 1.2 fusion.30
  104.6 0.7 compare_reduce_fusion.2
  105.3 1.3 %select_reduce_fusion.2 = (f32[80]{0:T(128)S(1)}, f32[80,1280]{1,0:T(8,128)S(1)}) fusion(pred[1280]{0:T(1024)(128)(4,1)S(1)} %compare_reduce_fusion.2, bf16[12,1280,64]{1,2,0:T(8,128)(2,1)} %get-tuple-element.169, s32[]{:T(128)} %get-tuple-element.156, bf16[12,80,64]{1,2,0:T(8,128)(2,1)S(1)} %get-tuple-element.168), kind=kOutput, calls=%fused_computation.6.clone.1 | convolution fusion | flops 13414320 | bytes 593216 | tf_op jit(solution)/shard_map/while/body/eval_jaxpr/dot_general | solution.py:33
  106.6 0.2 fusion.29
  106.9 1.2 fusion.30
  108.1 0.7 compare_reduce_fusion.2
  108.8 1.3 %select_reduce_fusion.2 = (f32[80]{0:T(128)S(1)}, f32[80,1280]{1,0:T(8,128)S(1)}) fusion(pred[1280]{0:T(1024)(128)(4,1)S(1)} %compare_reduce_fusion.2, bf16[12,1280,64]{1,2,0:T(8,128)(2,1)} %get-tuple-element.169, s32[]{:T(128)} %get-tuple-element.156, bf16[12,80,64]{1,2,0:T(8,128)(2,1)S(1)} %get-tuple-element.168), kind=kOutput, calls=%fused_computation.6.clone.1 | convolution fusion | flops 13414320 | bytes 593216 | tf_op jit(solution)/shard_map/while/body/eval_jaxpr/dot_general | solution.py:33
  110.1 0.2 fusion.29
  110.3 1.2 fusion.30
  111.6 0.7 compare_reduce_fusion.2
  112.3 1.3 %select_reduce_fusion.2 = (f32[80]{0:T(128)S(1)}, f32[80,1280]{1,0:T(8,128)S(1)}) fusion(pred[1280]{0:T(1024)(128)(4,1)S(1)} %compare_reduce_fusion.2, bf16[12,1280,64]{1,2,0:T(8,128)(2,1)} %get-tuple-element.169, s32[]{:T(128)} %get-tuple-element.156, bf16[12,80,64]{1,2,0:T(8,128)(2,1)S(1)} %get-tuple-element.168), kind=kOutput, calls=%fused_computation.6.clone.1 | convolution fusion | flops 13414320 | bytes 593216 | tf_op jit(solution)/shard_map/while/body/eval_jaxpr/dot_general | solution.py:33
  113.5 0.2 fusion.29
  113.8 1.2 fusion.30
  115.1 0.1 fusion.19
  115.2 0.0 copy-done
  115.2 1.3 %convolution_convert_fusion = bf16[80,1536]{1,0:T(8,128)(2,1)} fusion(bf16[80,768]{0,1:T(8,128)(2,1)S(1)} %fusion.19, bf16[768,1536]{1,0:T(8,128)(2,1)S(1)} %copy-done), kind=kOutput, calls=%fused_computation.25 | convolution fusion | flops 188866560 | bytes 2727936 | tf_op jit(solution)/shard_map/dot_general | solution.py:54
  (40 shorter events, 0.7 us)
Async XLA Ops:
  6.5 108.6 %copy-start = (bf16[768,1536]{1,0:T(8,128)(2,1)S(1)}, bf16[768,1536]{1,0:T(8,128)(2,1)}, u32[]{:S(2)}) copy-start(bf16[768,1536]{1,0:T(8,128)(2,1)} %param.11) | copy-start | bytes 7077892
  6.5 54.6 %all-gather.2.cloned.1.call-start = ((), (), s32[]{:S(2)}) async-start(), calls=%async_computation | async-start | bytes 4177920 | tf_op jit(solution)/shard_map/all_gather | solution.py:22
Sparse Core Ops, SparseCore 0:
  9.6 51.4 all-gather.1
